TPU v7x, 512 devices: a whole 4x4x16 slice. The times are simulated.
512 devices in a mesh: dp: 8 (over y, z_hi), tensor: 64 (over x, z_lo, core).
Axes of the slice: x: 4, y: 4, z: 16 (z_hi: 2, z_lo: 8; z = z_hi * 8 + z_lo), core: 2. Of those that a mesh axis runs over, the one named last changes fastest.
Arguments:
- tokens: bfloat16 [8192, 8192], P('dp', 'tensor'), may hold values from -6 to 6
- first_up: bfloat16 [64, 128, 128], P('tensor'), may hold values from -0.5 to 0.5
- second_up: bfloat16 [128, 64, 256], P('tensor'), may hold values from -0.75 to 0.75
- first_down: bfloat16 [128, 256, 64], P('tensor'), may hold values from -0.375 to 0.375
- second_down: bfloat16 [64, 128, 128], P('tensor'), may hold values from -0.5 to 0.5
- out_grad: bfloat16 [8192, 8192], P('dp', 'tensor'), may hold values from -6 to 6
Outputs:
- output: bfloat16 [8192, 8192], P('dp', 'tensor')
- tokens_grad: bfloat16 [8192, 8192], P('dp', 'tensor')
- first_up_grad: float32 [64, 128, 128], P('tensor')
- second_up_grad: float32 [128, 64, 256], P('tensor')
- first_down_grad: float32 [128, 256, 64], P('tensor')
- second_down_grad: float32 [64, 128, 128], P('tensor')
All inputs are finite; a program needn't handle non-finite values.
Results may differ from a plain program's by a relative error of at most 0.0095.
Values may be sent and summed in bfloat16 or wider, within the bound.
A program may use at most 64 MiB of HBM per device.

v0:
```python
import math
import jax
import jax.numpy as jnp
from jax import lax
from jax.sharding import PartitionSpec as P


def cdf_part(value):
    return 0.5 * (1.0 + jax.scipy.special.erf(value / math.sqrt(2.0)))


def gelu_deriv(value):
    return cdf_part(value) + value * jnp.exp(-0.5 * value * value) / math.sqrt(2.0 * math.pi)


def middle_work(upper_cols, second_up, first_down):
    f32 = jnp.float32
    bf16 = jnp.bfloat16
    pre = jnp.einsum("jbt,jbo->jot", upper_cols, second_up, preferred_element_type=f32).astype(bf16)
    prefl = pre.astype(f32)
    act = (prefl * cdf_part(prefl)).astype(bf16)
    zeta = jnp.einsum("jot,job->jbt", act, first_down, preferred_element_type=f32).astype(bf16)
    return (pre, act, zeta)


def column_backward(dzeta_cols, act, pre, upper_cols, second_up, first_down):
    f32 = jnp.float32
    bf16 = jnp.bfloat16
    grad_d1 = jnp.einsum("jot,jbt->job", act, dzeta_cols, preferred_element_type=f32)
    dact = jnp.einsum("jbt,job->jot", dzeta_cols, first_down, preferred_element_type=f32)
    dpre = (dact * gelu_deriv(pre.astype(f32))).astype(bf16)
    grad_u2 = jnp.einsum("jbt,jot->jbo", upper_cols, dpre, preferred_element_type=f32)
    dupper = jnp.einsum("jot,jbo->jbt", dpre, second_up, preferred_element_type=f32).astype(bf16)
    return (grad_d1, grad_u2, dupper)


def shards(tokens, first_up, second_up, first_down, second_down, out_grad):
    f32 = jnp.float32
    bf16 = jnp.bfloat16
    tok_rows = tokens.shape[0]
    local_blocks = first_up.shape[0]
    blk_width = first_up.shape[1]
    xblk = tokens.reshape(tok_rows, local_blocks, blk_width)
    eblk = out_grad.reshape(tok_rows, local_blocks, blk_width)
    upper = jnp.einsum("tbi,bij->jbt", xblk, first_up, preferred_element_type=f32).astype(bf16)
    upper_cols = lax.all_to_all(upper, "tensor", split_axis=0, concat_axis=1, tiled=True)
    pre, act, zeta = middle_work(upper_cols, second_up, first_down)
    zeta_rows = lax.all_to_all(zeta, "tensor", split_axis=1, concat_axis=0, tiled=True)
    grad_d2 = jnp.einsum("jbt,tbk->bjk", zeta_rows, eblk, preferred_element_type=f32)
    dzeta = jnp.einsum("tbk,bjk->jbt", eblk, second_down, preferred_element_type=f32).astype(bf16)
    dzeta_cols = lax.all_to_all(dzeta, "tensor", split_axis=0, concat_axis=1, tiled=True)
    grad_d1, grad_u2, dupper = column_backward(
        dzeta_cols, act, pre, upper_cols, second_up, first_down
    )
    dupper_rows = lax.all_to_all(dupper, "tensor", split_axis=1, concat_axis=0, tiled=True)
    output = jnp.einsum("jbt,bjk->tbk", zeta_rows, second_down, preferred_element_type=f32).astype(
        bf16
    )
    output = output.reshape(tok_rows, local_blocks * blk_width)
    grad_u1 = jnp.einsum("tbi,jbt->bij", xblk, dupper_rows, preferred_element_type=f32)
    grad_u1, grad_u2, grad_d1, grad_d2 = lax.psum((grad_u1, grad_u2, grad_d1, grad_d2), "dp")
    tokens_grad = jnp.einsum(
        "jbt,bij->tbi", dupper_rows, first_up, preferred_element_type=f32
    ).astype(bf16)
    tokens_grad = tokens_grad.reshape(tok_rows, local_blocks * blk_width)
    return (output, tokens_grad, grad_u1, grad_u2, grad_d1, grad_d2)


def solution(mesh):
    placed = (
        P("dp", "tensor"),
        P("tensor", None, None),
        P("tensor", None, None),
        P("tensor", None, None),
        P("tensor", None, None),
        P("dp", "tensor"),
    )
    return jax.shard_map(
        shards,
        mesh=mesh,
        in_specs=placed,
        out_specs=(
            P("dp", "tensor"),
            P("dp", "tensor"),
            P("tensor", None, None),
            P("tensor", None, None),
            P("tensor", None, None),
            P("tensor", None, None),
        ),
        check_vma=False,
    )
```

profile of v0, /device:TPU:102, one launch (start us, length us, event | category | flops | bytes accessed | tf_op | source)
XLA Modules:
  0.0 323.2 jit_solution(2137689660007310916)
XLA Ops:
  8.1 1.0 fusion.12
  11.2 14.9 %all-to-all-start = ((bf16[64,2,1024]{2,1,0:T(2,128)(2,1)}), bf16[64,2,1024]{2,1,0:T(2,128)(2,1)S(1)}, u32[]{:S(2)}, u32[]{:S(2)}) async-start(bf16[64,2,1024]{2,1,0:T(2,128)(2,1)} %reshape.62), calls=%async_computation | async-start | bytes 524288 | tf_op jit(solution)/shard_map/all_to_all | solution.py:46
  28.0 13.2 %all-to-all-done = bf16[64,2,1024]{2,1,0:T(2,128)(2,1)S(1)} async-done(((bf16[64,2,1024]{2,1,0:T(2,128)(2,1)}), bf16[64,2,1024]{2,1,0:T(2,128)(2,1)S(1)}, u32[]{:S(2)}, u32[]{:S(2)}) %all-to-all-start) | async-done | bytes 262176 | tf_op jit(solution)/shard_map/all_to_all | solution.py:46
  41.2 11.1 %all-to-all-start.2 = ((bf16[64,2,1024]{2,1,0:T(2,128)(2,1)}), bf16[64,2,1024]{2,1,0:T(2,128)(2,1)S(1)}, u32[]{:S(2)}, u32[]{:S(2)}) async-start(bf16[64,2,1024]{2,1,0:T(2,128)(2,1)} %reshape.64), calls=%async_computation.2 | async-start | bytes 524288 | tf_op jit(solution)/shard_map/all_to_all | solution.py:51
  52.6 1.5 reduce
  54.9 12.5 %all-to-all-done.2 = bf16[64,2,1024]{2,1,0:T(2,128)(2,1)S(1)} async-done(((bf16[64,2,1024]{2,1,0:T(2,128)(2,1)}), bf16[64,2,1024]{2,1,0:T(2,128)(2,1)S(1)}, u32[]{:S(2)}, u32[]{:S(2)}) %all-to-all-start.2) | async-done | bytes 262176 | tf_op jit(solution)/shard_map/all_to_all | solution.py:51
  67.6 1.5 reduce.1
  70.0 1.5 fusion.8
  74.7 11.3 %all-to-all-start.3 = ((bf16[2,64,1024]{2,0,1:T(2,128)(2,1)}), bf16[2,64,1024]{2,0,1:T(2,128)(2,1)}, u32[]{:S(2)}, u32[]{:S(2)}) async-start(bf16[2,64,1024]{2,0,1:T(2,128)(2,1)} %copy.44), calls=%async_computation.3 | async-start | bytes 524288 | tf_op jit(solution)/shard_map/all_to_all | solution.py:55
  86.1 1.3 fusion.10
  87.3 1.0 copy.40
  88.3 12.7 %all-to-all-done.3 = bf16[2,64,1024]{2,0,1:T(2,128)(2,1)} async-done(((bf16[2,64,1024]{2,0,1:T(2,128)(2,1)}), bf16[2,64,1024]{2,0,1:T(2,128)(2,1)}, u32[]{:S(2)}, u32[]{:S(2)}) %all-to-all-start.3) | async-done | bytes 262176 | tf_op jit(solution)/shard_map/all_to_all | solution.py:55
  101.0 11.3 %all-to-all-start.1 = ((bf16[2,64,1024]{2,0,1:T(2,128)(2,1)}), bf16[2,64,1024]{2,0,1:T(2,128)(2,1)}, u32[]{:S(2)}, u32[]{:S(2)}) async-start(bf16[2,64,1024]{2,0,1:T(2,128)(2,1)} %copy.40), calls=%async_computation.1 | async-start | bytes 524288 | tf_op jit(solution)/shard_map/all_to_all | solution.py:48
  112.4 2.3 fusion.17
  114.7 2.0 fusion.14
  116.6 1.1 reshape.59
  118.5 8.8 %all-to-all-done.1 = bf16[2,64,1024]{2,0,1:T(2,128)(2,1)} async-done(((bf16[2,64,1024]{2,0,1:T(2,128)(2,1)}), bf16[2,64,1024]{2,0,1:T(2,128)(2,1)}, u32[]{:S(2)}, u32[]{:S(2)}) %all-to-all-start.1) | async-done | bytes 262176 | tf_op jit(solution)/shard_map/all_to_all | solution.py:48
  127.3 1.0 reshape.57
  128.4 1.8 convolution_bitcast_fusion
  132.1 178.1 %all-reduce.3.cloned.1.call-done = (f32[1,128,128]{1,2,0:T(8,128)}, f32[2,64,256]{2,1,0:T(8,128)}, f32[2,256,64]{1,2,0:T(8,128)}, f32[1,128,128]{2,1,0:T(8,128)}) async-done(((f32[1,128,128]{1,2,0:T(8,128)}, f32[2,64,256]{2,1,0:T(8,128)}, f32[2,256,64]{1,2,0:T(8,128)}, f32[1,128,128]{2,1,0:T(8,128)}), (f32[1,128,128]{1,2,0:T(8,128)}, f32[2,64,256]{2,1,0:T(8,128)}, f32[2,256,64]{1,2,0:T(8,128)}, ...) | async-done | bytes 393232 | tf_op jit(solution)/shard_map/psum | solution.py:61
  310.2 1.6 copy.47
  311.8 1.6 copy.80
  313.4 1.6 copy.81
  314.9 1.5 copy.82
  (34 shorter events, 13.0 us)
Async XLA Ops:
  7.2 1.0 copy-start
  7.2 19.0 %copy-start.6 = (bf16[1,128,128]{2,1,0:T(8,128)(2,1)S(1)}, bf16[1,128,128]{2,1,0:T(8,128)(2,1)}, u32[]{:S(2)}) copy-start(bf16[1,128,128]{2,1,0:T(8,128)(2,1)} %param.10) | copy-start | bytes 98308
  7.2 19.0 %copy-start.3 = (bf16[1024,128]{1,0:T(8,128)(2,1)S(1)}, bf16[1024,128]{1,0:T(8,128)(2,1)}, u32[]{:S(2)}) copy-start(bf16[1024,128]{1,0:T(8,128)(2,1)} %param.11) | copy-start | bytes 786436
  11.2 30.0 %all-to-all-start = ((bf16[64,2,1024]{2,1,0:T(2,128)(2,1)}), bf16[64,2,1024]{2,1,0:T(2,128)(2,1)S(1)}, u32[]{:S(2)}, u32[]{:S(2)}) async-start(bf16[64,2,1024]{2,1,0:T(2,128)(2,1)} %reshape.62), calls=%async_computation | async-start | bytes 524288 | tf_op jit(solution)/shard_map/all_to_all | solution.py:46
  41.2 26.2 %all-to-all-start.2 = ((bf16[64,2,1024]{2,1,0:T(2,128)(2,1)}), bf16[64,2,1024]{2,1,0:T(2,128)(2,1)S(1)}, u32[]{:S(2)}, u32[]{:S(2)}) async-start(bf16[64,2,1024]{2,1,0:T(2,128)(2,1)} %reshape.64), calls=%async_computation.2 | async-start | bytes 524288 | tf_op jit(solution)/shard_map/all_to_all | solution.py:51
  52.3 17.6 %copy-start.4 = (bf16[2,64,256]{2,1,0:T(8,128)(2,1)S(1)}, bf16[2,64,256]{2,1,0:T(8,128)(2,1)}, u32[]{:S(2)}) copy-start(bf16[2,64,256]{2,1,0:T(8,128)(2,1)} %param.8) | copy-start | bytes 196612
  69.9 1.6 copy-start.2
  70.0 1.6 copy-start.7
  72.4 1.0 copy-start.1
  74.7 26.3 %all-to-all-start.3 = ((bf16[2,64,1024]{2,0,1:T(2,128)(2,1)}), bf16[2,64,1024]{2,0,1:T(2,128)(2,1)}, u32[]{:S(2)}, u32[]{:S(2)}) async-start(bf16[2,64,1024]{2,0,1:T(2,128)(2,1)} %copy.44), calls=%async_computation.3 | async-start | bytes 524288 | tf_op jit(solution)/shard_map/all_to_all | solution.py:55
  101.0 26.3 %all-to-all-start.1 = ((bf16[2,64,1024]{2,0,1:T(2,128)(2,1)}), bf16[2,64,1024]{2,0,1:T(2,128)(2,1)}, u32[]{:S(2)}, u32[]{:S(2)}) async-start(bf16[2,64,1024]{2,0,1:T(2,128)(2,1)} %copy.40), calls=%async_computation.1 | async-start | bytes 524288 | tf_op jit(solution)/shard_map/all_to_all | solution.py:48
  112.3 197.9 %all-reduce.3.cloned.1.call-start = ((), (), s32[]{:S(2)}) async-start(), calls=%async_computation.4 | async-start | bytes 786432 | tf_op jit(solution)/shard_map/psum | solution.py:61
  116.6 13.6 %copy-start.5 = (bf16[1,128,128]{2,1,0:T(8,128)(2,1)S(1)}, bf16[1,128,128]{2,1,0:T(8,128)(2,1)}, u32[]{:S(2)}) copy-start(bf16[1,128,128]{2,1,0:T(8,128)(2,1)} %param.7) | copy-start | bytes 98308
Sparse Core Ops, SparseCore 0:
  130.3 179.8 all-reduce.2
where the time goes:
time: 324 us; the launch traced here: 323 us
  waiting for transfers between devices  225 us (69%)
  starting transfers between devices  48.7 us (15%)
  local copies, waits for them, and re-layouts  16.3 us (5%)
  between operations  14.2 us (4%)
  matrix products  14.1 us (4%)
  other arithmetic  4.59 us (1%)
    psum x1, waiting for transfers between devices, shards(): lax.psum((grad_u1, grad_u2, grad_d1, grad_d2), 'dp')  178 us
    all_to_all x1, starting transfers between devices, shards(): lax.all_to_all(upper, 'tensor', split_axis=0, concat_axis=1, tiled=True)  14.9 us
    all_to_all x1, waiting for transfers between devices, shards(): lax.all_to_all(upper, 'tensor', split_axis=0, concat_axis=1, tiled=True)  13.2 us
    all_to_all x1, waiting for transfers between devices, shards(): lax.all_to_all(dupper, 'tensor', split_axis=1, concat_axis=0, tiled=True)  12.7 us
    all_to_all x1, waiting for transfers between devices, shards(): lax.all_to_all(dzeta, 'tensor', split_axis=0, concat_axis=1, tiled=True)  12.5 us
    all_to_all x1, starting transfers between devices, shards(): lax.all_to_all(dupper, 'tensor', split_axis=1, concat_axis=0, tiled=True)  11.3 us
    all_to_all x1, starting transfers between devices, shards(): lax.all_to_all(zeta, 'tensor', split_axis=1, concat_axis=0, tiled=True)  11.3 us
    all_to_all x1, starting transfers between devices, shards(): lax.all_to_all(dzeta, 'tensor', split_axis=0, concat_axis=1, tiled=True)  11.1 us
  transfers between devices with their start and end apart: 5, of which 5 were waited for; matrix products, arithmetic and copies ran while one was open for 4% of the time, Pallas kernels for 0%

commit v1 on v0

--- a/solution.py
+++ b/solution.py
@@ -3,6 +3,7 @@
 import jax.numpy as jnp
 from jax import lax
 from jax.sharding import PartitionSpec as P
+from jax.lax import all_to_all, psum
 
 
 def cdf_part(value):
@@ -35,6 +36,19 @@
 
 
 def shards(tokens, first_up, second_up, first_down, second_down, out_grad):
+
+    def pair_tables_here(x_local, along_axis, out_dim, dim_at=1):
+        local_now = jnp.concatenate(
+            all_to_all(
+                jnp.stack(jnp.split(x_local, psum(1, axis_name=along_axis), axis=out_dim), axis=0),
+                axis_name=along_axis,
+                split_axis=0,
+                concat_axis=0,
+            ),
+            dim_at,
+        )
+        return local_now
+
     f32 = jnp.float32
     bf16 = jnp.bfloat16
     tok_rows = tokens.shape[0]
@@ -48,7 +62,7 @@
     zeta_rows = lax.all_to_all(zeta, "tensor", split_axis=1, concat_axis=0, tiled=True)
     grad_d2 = jnp.einsum("jbt,tbk->bjk", zeta_rows, eblk, preferred_element_type=f32)
     dzeta = jnp.einsum("tbk,bjk->jbt", eblk, second_down, preferred_element_type=f32).astype(bf16)
-    dzeta_cols = lax.all_to_all(dzeta, "tensor", split_axis=0, concat_axis=1, tiled=True)
+    dzeta_cols = pair_tables_here(dzeta, "tensor", 0)
     grad_d1, grad_u2, dupper = column_backward(
         dzeta_cols, act, pre, upper_cols, second_up, first_down
     )

time: 324 us -> 347 us (1.071)
  local copies, waits for them, and re-layouts: 16.3 us -> 52.8 us
  waiting for transfers between devices: 225 us -> 211 us
    unnamed x24 -> x81, local copies, waits for them, and re-layouts: 10.2 us -> 46.8 us
    all_to_all x1, waiting for transfers between devices: 13.2 us -> 0.01 us  [shards(): lax.all_to_all(upper, 'tensor', split_axis=0, concat_axis=1, tiled=True)]
  transfers between devices with their start and end apart: 5 -> 5, of which waited for: 5 -> 4; matrix products, arithmetic and copies ran while one was open for 4% -> 15% of each run, Pallas kernels for 0% -> 0%
where the time goes in v1:
time: 347 us; the launch traced here: 346 us
  waiting for transfers between devices  211 us (61%)
  local copies, waits for them, and re-layouts  52.8 us (15%)
  starting transfers between devices  50.9 us (15%)
  matrix products  15 us (4%)
  between operations  14.2 us (4%)
    psum x1, waiting for transfers between devices, shards(): lax.psum((grad_u1, grad_u2, grad_d1, grad_d2), 'dp')  178 us
    unnamed x81, local copies, waits for them, and re-layouts  46.8 us
    all_to_all x1, starting transfers between devices, shards(): lax.all_to_all(upper, 'tensor', split_axis=0, concat_axis=1, tiled=True)  15 us
    all_to_all x1, starting transfers between devices, pair_tables_here(): all_to_all(jnp.stack(jnp.split(x_local, psum(1, axis_name=along_axis), ax...  13.3 us
    all_to_all x1, waiting for transfers between devices, shards(): lax.all_to_all(dupper, 'tensor', split_axis=1, concat_axis=0, tiled=True)  12.7 us
    all_to_all x1, starting transfers between devices, shards(): lax.all_to_all(zeta, 'tensor', split_axis=1, concat_axis=0, tiled=True)  11.3 us
    all_to_all x1, starting transfers between devices, shards(): lax.all_to_all(dupper, 'tensor', split_axis=1, concat_axis=0, tiled=True)  11.3 us
    all_to_all x1, waiting for transfers between devices, pair_tables_here(): all_to_all(jnp.stack(jnp.split(x_local, psum(1, axis_name=along_axis), ax...  10.9 us
  transfers between devices with their start and end apart: 5, of which 4 were waited for; matrix products, arithmetic and copies ran while one was open for 15% of the time, Pallas kernels for 0%

profile of v1, /device:TPU:102, one launch (start us, length us, event | category | flops | bytes accessed | tf_op | source)
XLA Modules:
  0.0 346.1 jit_solution(13217377398322833098)
XLA Ops:
  8.1 1.0 fusion.12
  11.2 15.0 %all-to-all-start = ((bf16[64,2,1024]{2,1,0:T(2,128)(2,1)}), bf16[64,2,1024]{2,1,0:T(2,128)(2,1)S(1)}, u32[]{:S(2)}, u32[]{:S(2)}) async-start(bf16[64,2,1024]{2,1,0:T(2,128)(2,1)} %reshape.197), calls=%async_computation | async-start | bytes 524288 | tf_op jit(solution)/shard_map/all_to_all | solution.py:60
  64.9 13.3 %all-to-all-start.2 = ((bf16[64,2,1,1024]{3,1,2,0:T(2,128)(2,1)}), bf16[64,2,1,1024]{3,1,2,0:T(2,128)(2,1)}, u32[]{:S(2)}, u32[]{:S(2)}) async-start(bf16[64,2,1,1024]{3,1,2,0:T(2,128)(2,1)} %constant_dynamic-update-slice_fusion), calls=%async_computation.2 | async-start | bytes 524288 | tf_op jit(solution)/shard_map/all_to_all | solution.py:42
  78.4 1.5 reduce
  80.7 1.5 fusion.8
  82.2 10.9 %all-to-all-done.2 = bf16[64,2,1,1024]{3,1,2,0:T(2,128)(2,1)} async-done(((bf16[64,2,1,1024]{3,1,2,0:T(2,128)(2,1)}), bf16[64,2,1,1024]{3,1,2,0:T(2,128)(2,1)}, u32[]{:S(2)}, u32[]{:S(2)}) %all-to-all-start.2) | async-done | bytes 262176 | tf_op jit(solution)/shard_map/all_to_all | solution.py:42
  93.1 1.8 fusion.5
  96.3 1.0 copy.46
  97.3 11.3 %all-to-all-start.3 = ((bf16[2,64,1024]{2,0,1:T(2,128)(2,1)}), bf16[2,64,1024]{2,0,1:T(2,128)(2,1)}, u32[]{:S(2)}, u32[]{:S(2)}) async-start(bf16[2,64,1024]{2,0,1:T(2,128)(2,1)} %copy.46), calls=%async_computation.3 | async-start | bytes 524288 | tf_op jit(solution)/shard_map/all_to_all | solution.py:69
  108.6 1.3 fusion.10
  109.9 1.0 copy.43
  110.9 12.7 %all-to-all-done.3 = bf16[2,64,1024]{2,0,1:T(2,128)(2,1)} async-done(((bf16[2,64,1024]{2,0,1:T(2,128)(2,1)}), bf16[2,64,1024]{2,0,1:T(2,128)(2,1)}, u32[]{:S(2)}, u32[]{:S(2)}) %all-to-all-start.3) | async-done | bytes 262176 | tf_op jit(solution)/shard_map/all_to_all | solution.py:69
  123.6 11.3 %all-to-all-start.1 = ((bf16[2,64,1024]{2,0,1:T(2,128)(2,1)}), bf16[2,64,1024]{2,0,1:T(2,128)(2,1)}, u32[]{:S(2)}, u32[]{:S(2)}) async-start(bf16[2,64,1024]{2,0,1:T(2,128)(2,1)} %copy.43), calls=%async_computation.1 | async-start | bytes 524288 | tf_op jit(solution)/shard_map/all_to_all | solution.py:62
  134.9 2.3 fusion.13
  137.2 2.0 fusion.16
  139.2 1.1 reshape.195
  141.1 8.8 %all-to-all-done.1 = bf16[2,64,1024]{2,0,1:T(2,128)(2,1)} async-done(((bf16[2,64,1024]{2,0,1:T(2,128)(2,1)}), bf16[2,64,1024]{2,0,1:T(2,128)(2,1)}, u32[]{:S(2)}, u32[]{:S(2)}) %all-to-all-start.1) | async-done | bytes 262176 | tf_op jit(solution)/shard_map/all_to_all | solution.py:62
  149.9 1.0 reshape.191
  150.9 1.8 convolution_bitcast_fusion
  154.7 178.4 %all-reduce.3.cloned.1.call-done = (f32[1,128,128]{1,2,0:T(8,128)}, f32[2,64,256]{2,1,0:T(8,128)}, f32[2,256,64]{1,2,0:T(8,128)}, f32[1,128,128]{2,1,0:T(8,128)}) async-done(((f32[1,128,128]{1,2,0:T(8,128)}, f32[2,64,256]{2,1,0:T(8,128)}, f32[2,256,64]{1,2,0:T(8,128)}, f32[1,128,128]{2,1,0:T(8,128)}), (f32[1,128,128]{1,2,0:T(8,128)}, f32[2,64,256]{2,1,0:T(8,128)}, f32[2,256,64]{1,2,0:T(8,128)}, ...) | async-done | bytes 393232 | tf_op jit(solution)/shard_map/psum | solution.py:75
  333.1 1.6 copy.50
  334.6 1.6 copy.139
  336.2 1.6 copy.140
  337.8 1.5 copy.141
  (89 shorter events, 46.8 us)
Async XLA Ops:
  7.2 1.0 copy-start
  7.2 19.1 %copy-start.5 = (bf16[1,128,128]{2,1,0:T(8,128)(2,1)S(1)}, bf16[1,128,128]{2,1,0:T(8,128)(2,1)}, u32[]{:S(2)}) copy-start(bf16[1,128,128]{2,1,0:T(8,128)(2,1)} %param.10) | copy-start | bytes 98308
  7.2 19.1 %copy-start.2 = (bf16[1024,128]{1,0:T(8,128)(2,1)S(1)}, bf16[1024,128]{1,0:T(8,128)(2,1)}, u32[]{:S(2)}) copy-start(bf16[1024,128]{1,0:T(8,128)(2,1)} %param.11) | copy-start | bytes 786436
  11.2 69.5 %copy-start.3 = (bf16[2,64,256]{2,1,0:T(8,128)(2,1)S(1)}, bf16[2,64,256]{2,1,0:T(8,128)(2,1)}, u32[]{:S(2)}) copy-start(bf16[2,64,256]{2,1,0:T(8,128)(2,1)} %param.8) | copy-start | bytes 196612
  11.2 53.6 %all-to-all-start = ((bf16[64,2,1024]{2,1,0:T(2,128)(2,1)}), bf16[64,2,1024]{2,1,0:T(2,128)(2,1)S(1)}, u32[]{:S(2)}, u32[]{:S(2)}) async-start(bf16[64,2,1024]{2,1,0:T(2,128)(2,1)} %reshape.197), calls=%async_computation | async-start | bytes 524288 | tf_op jit(solution)/shard_map/all_to_all | solution.py:60
  64.9 28.2 %all-to-all-start.2 = ((bf16[64,2,1,1024]{3,1,2,0:T(2,128)(2,1)}), bf16[64,2,1,1024]{3,1,2,0:T(2,128)(2,1)}, u32[]{:S(2)}, u32[]{:S(2)}) async-start(bf16[64,2,1,1024]{3,1,2,0:T(2,128)(2,1)} %constant_dynamic-update-slice_fusion), calls=%async_computation.2 | async-start | bytes 524288 | tf_op jit(solution)/shard_map/all_to_all | solution.py:42
  94.9 1.0 copy-start.1
  97.3 26.3 %all-to-all-start.3 = ((bf16[2,64,1024]{2,0,1:T(2,128)(2,1)}), bf16[2,64,1024]{2,0,1:T(2,128)(2,1)}, u32[]{:S(2)}, u32[]{:S(2)}) async-start(bf16[2,64,1024]{2,0,1:T(2,128)(2,1)} %copy.46), calls=%async_computation.3 | async-start | bytes 524288 | tf_op jit(solution)/shard_map/all_to_all | solution.py:69
  123.6 26.3 %all-to-all-start.1 = ((bf16[2,64,1024]{2,0,1:T(2,128)(2,1)}), bf16[2,64,1024]{2,0,1:T(2,128)(2,1)}, u32[]{:S(2)}, u32[]{:S(2)}) async-start(bf16[2,64,1024]{2,0,1:T(2,128)(2,1)} %copy.43), calls=%async_computation.1 | async-start | bytes 524288 | tf_op jit(solution)/shard_map/all_to_all | solution.py:62
  134.9 198.2 %all-reduce.3.cloned.1.call-start = ((), (), s32[]{:S(2)}) async-start(), calls=%async_computation.4 | async-start | bytes 786432 | tf_op jit(solution)/shard_map/psum | solution.py:75
  139.2 13.6 %copy-start.4 = (bf16[1,128,128]{2,1,0:T(8,128)(2,1)S(1)}, bf16[1,128,128]{2,1,0:T(8,128)(2,1)}, u32[]{:S(2)}) copy-start(bf16[1,128,128]{2,1,0:T(8,128)(2,1)} %param.7) | copy-start | bytes 98308
Sparse Core Ops, SparseCore 0:
  152.9 180.1 all-reduce.2
